TPU v7x, 32 devices: a whole 2x2x4 slice. The times are simulated.
32 devices in a mesh: day: 2 (over y), stu: 16 (over z, x, core).
Axes of the slice: x: 2, y: 2, z: 4, core: 2. Of those that a mesh axis runs over, the one named last changes fastest.
Arguments:
- performance: bfloat16 [64, 128, 1024], P('day', 'stu'), may hold values from -8 to 8
- student_factor: bfloat16 [128, 256], P('stu'), may hold values from -0.5 to 0.5
- skill_factor: bfloat16 [1024, 256], replicated, may hold values from -0.1875 to 0.1875
- day_prev: float32 [64, 256], P('day'), may hold values from -6 to 6
- ar_coef: float32 [7], replicated, may hold values from -0.3 to 0.3
Outputs:
- day_factor: float32 [64, 256], P('day', 'stu')
- residual: float32 [64, 256], P('day', 'stu')
All inputs are finite; a program needn't handle non-finite values.
Results may differ from a plain program's by a relative error of at most 0.0003.
Values sent between devices are 32-bit elements; how exact they have to be, the bound alone decides.
No kernel may reach another device: no remote copies, remote signals or barrier semaphores. Data moves between devices by JAX's collectives and lax.ppermute only.
A program may use at most 64 MiB of HBM per device.

v0:
```python
import jax
import jax.numpy as jnp
from jax import lax
from jax.sharding import PartitionSpec as P

LAGS = 7
ITERS = 3
smoothing = 1.0


def shifted(block, axis, distance):
    devices = range(lax.axis_size(axis))
    route = [(i - distance, i) for i in devices if i - distance in devices]
    return lax.ppermute(block, axis, route)


def filter_rows(extended, coef, count):
    out = extended[LAGS : LAGS + count]
    for lag in range(1, LAGS + 1):
        out = out - coef[lag - 1] * extended[LAGS - lag : LAGS - lag + count]
    return out


def smooth(values, coef):
    count = values.shape[0]
    below = shifted(values[count - LAGS :], "day", 1)
    ahead_core = filter_rows(jnp.concatenate([below, values], 0), coef, count)
    above = shifted(ahead_core[:LAGS], "day", -1)
    ahead = jnp.concatenate([ahead_core, above], 0)
    out = ahead[:count]
    for lag in range(1, LAGS + 1):
        out = out - coef[lag - 1] * ahead[lag : lag + count]
    return out


def with_gram(values, gram_part):
    return jnp.dot(
        lax.all_gather(values, "stu", axis=1, tiled=True),
        gram_part,
        precision=lax.Precision.HIGHEST,
        preferred_element_type=jnp.float32,
    )


def operate(values, gram_part, coef):
    return with_gram(values, gram_part) + smoothing * smooth(values, coef)


def global_total(value):
    return lax.psum(value, ("day", "stu"))


def summed_gram(local_gram):
    return lax.psum(local_gram, "stu")


def local(performance, student_factor, skill_factor, day_prev, ar_coef):
    days, students, skills = performance.shape
    rank = skill_factor.shape[1]
    proj = jnp.dot(
        performance.reshape(days * students, skills),
        skill_factor,
        preferred_element_type=jnp.float32,
    )
    proj = proj.reshape(days, students, rank)
    local_terms = jnp.sum(proj * student_factor.astype(jnp.float32)[None], axis=1)
    local_gram = jnp.dot(student_factor.T, student_factor, preferred_element_type=jnp.float32)
    skill_gram = jnp.dot(skill_factor.T, skill_factor, preferred_element_type=jnp.float32)
    columns = rank // lax.axis_size("stu")
    first_col = lax.axis_index("stu") * columns
    gram = summed_gram(local_gram) * skill_gram
    mttkrp = lax.psum_scatter(local_terms, "stu", scatter_dimension=1, tiled=True)
    gram_part = lax.dynamic_slice_in_dim(gram, first_col, columns, 1)
    day_factor = lax.dynamic_slice_in_dim(day_prev, first_col, columns, 1)
    residual = mttkrp - operate(day_factor, gram_part, ar_coef)
    direction = residual
    norm_now = global_total(jnp.sum(residual * residual))
    for step in range(ITERS):
        image = operate(direction, gram_part, ar_coef)
        alpha = norm_now / global_total(jnp.sum(direction * image))
        day_factor = day_factor + alpha * direction
        residual = residual - alpha * image
        norm_next = global_total(jnp.sum(residual * residual))
        direction = residual + norm_next / norm_now * direction
        norm_now = norm_next
    return (day_factor, residual)


def solution(mesh):
    return jax.shard_map(
        local,
        mesh=mesh,
        in_specs=(P("day", "stu", None), P("stu", None), P(), P("day", None), P()),
        out_specs=(P("day", "stu"), P("day", "stu")),
        check_vma=False,
    )
```

profile of v0, /device:TPU:14, one launch (start us, length us, event | category | flops | bytes accessed | tf_op | source)
XLA Modules:
  0.0 491.8 jit_solution(908321572501885240)
XLA Ops:
  7.2 0.9 constant_dynamic-slice_fusion
  8.1 0.1 copy.10
  8.2 0.1 slice.333
  8.3 1.3 collective-permute-start
  9.6 1.7 fusion.139
  11.3 0.0 reduce-scatter.2.cloned.1.call-start
  11.3 0.6 copy-done.2
  11.9 0.3 fusion
  12.3 0.8 copy.9
  13.1 0.3 fusion.140
  13.4 0.3 copy-done.3
  13.7 0.7 fusion.138
  14.3 15.5 %all_gather.12 = f32[32,256]{0,1:T(8,128)S(1)} all-gather(f32[32,16]{0,1:T(8,128)S(1)} %copy.10), channel_id=1, replica_groups=mesh['day'=2,'stu'=16] {'stu'}, dimensions={1}, use_global_device_ids=true | all-gather | bytes 34816 | tf_op jit(solution)/shard_map/all_gather | solution.py:38
  29.8 4.5 fusion.120
  34.3 4.6 collective-permute-start.1
  38.9 64.2 %all-reduce.3.cloned.1.call-done = f32[256,256]{0,1:T(8,128)} async-done(((f32[256,256]{0,1:T(8,128)}), f32[256,256]{0,1:T(8,128)}) %all-reduce.3.cloned.1.call-update) | async-done | bytes 262160 | tf_op jit(solution)/shard_map/psum | solution.py:54
  103.1 0.7 dynamic-slice_multiply_fusion
  103.8 57.7 %reduce-scatter.2.cloned.1.call-done = f32[32,16]{0,1:T(8,128)} async-done(((f32[32,256]{0,1:T(8,128)}), f32[32,16]{0,1:T(8,128)}) %reduce-scatter.2.cloned.1.call-update) | async-done | bytes 2064 | tf_op jit(solution)/shard_map/reduce_scatter | solution.py:72
  161.5 5.2 %fusion.104 = f32[32,16]{0,1:T(8,128)S(1)} fusion(f32[32,16]{0,1:T(8,128)} %reduce-scatter.2.cloned.1.call-done, f32[7,16]{0,1:T(8,128)S(1)} %collective-permute-done.1, f32[32,16]{0,1:T(8,128)S(1)} %fusion.120, f32[]{:T(128)} %bitcast.7, f32[]{:T(128)} %bitcast.6, f32[]{:T(128)} %bitcast.5, f32[]{:T(128)} %bitcast.4, f32[]{:T(128)} %bitcast.3, ...), kind=kOutput, calls=%fused_computation.173 | convolution fusion | flops 1584640 | bytes 55772 | tf_op jit(solution)/shard_map/dot_general | solution.py:37
  166.7 0.1 slice.359
  166.8 1.3 collective-permute-start.2
  168.1 4.2 collective-permute-done.2
  172.3 4.5 fusion.86
  176.8 1.6 collective-permute-start.3
  178.5 15.4 %all_gather.13 = f32[32,256]{0,1:T(8,128)S(1)} all-gather(f32[32,16]{0,1:T(8,128)S(1)} %fusion.104), channel_id=1, replica_groups=mesh['day'=2,'stu'=16] {'stu'}, dimensions={1}, use_global_device_ids=true | all-gather | bytes 34816 | tf_op jit(solution)/shard_map/all_gather | solution.py:38
  193.8 5.2 %multiply_reduce_fusion.4 = (f32[]{:T(128)}, f32[]{:T(128)}, f32[32,16]{0,1:T(8,128)S(1)}) fusion(f32[32,16]{0,1:T(8,128)S(1)} %fusion.104, f32[7,16]{0,1:T(8,128)S(1)} %collective-permute-done.3, f32[32,16]{0,1:T(8,128)S(1)} %fusion.86, f32[]{:T(128)} %bitcast.7, f32[]{:T(128)} %bitcast.6, f32[]{:T(128)} %bitcast.5, f32[]{:T(128)} %bitcast.4, ...), kind=kOutput, calls=%fused_computation.235 | convolution fusion | flops 1586174 | bytes 55780 | tf_op jit(solution)/shard_map/dot_general | solution.py:37
  199.0 44.1 %all-reduce = (f32[]{:T(128)}, f32[]{:T(128)}) all-reduce(f32[]{:T(128)} %get-tuple-element.3, f32[]{:T(128)} %get-tuple-element.2), channel_id=1, replica_groups=mesh['day'=2,'stu'=16] {'day','stu'}, use_global_device_ids=true, to_apply=%region_4.0 | all-reduce | flops 2 | bytes 16 | tf_op jit(solution)/shard_map/psum | solution.py:50
  244.4 0.6 multiply_reduce_fusion.3
  245.1 38.6 %psum.52 = f32[]{:T(128)} all-reduce(f32[]{:T(128)} %multiply_reduce_fusion.3), channel_id=1, replica_groups=mesh['day'=2,'stu'=16] {'day','stu'}, use_global_device_ids=true, to_apply=%region_8.0 | all-reduce | flops 1 | bytes 8 | tf_op jit(solution)/shard_map/psum | solution.py:50
  285.1 0.1 slice.385
  285.1 1.3 collective-permute-start.4
  286.4 4.2 collective-permute-done.4
  290.7 4.5 fusion.53
  295.1 1.6 collective-permute-start.5
  296.8 18.0 %all_gather.14 = f32[32,256]{0,1:T(8,128)S(1)} all-gather(f32[32,16]{0,1:T(8,128)S(1)} %multiply_add_fusion.2), channel_id=1, replica_groups=mesh['day'=2,'stu'=16] {'stu'}, dimensions={1}, use_global_device_ids=true | all-gather | bytes 34816 | tf_op jit(solution)/shard_map/all_gather | solution.py:38
  314.8 5.2 %multiply_reduce_fusion.2 = (f32[]{:T(128)}, f32[32,16]{0,1:T(8,128)S(1)}) fusion(f32[32,16]{0,1:T(8,128)S(1)} %multiply_add_fusion.2, f32[7,16]{0,1:T(8,128)S(1)} %collective-permute-done.5, f32[32,16]{0,1:T(8,128)S(1)} %fusion.53, f32[]{:T(128)} %bitcast.7, f32[]{:T(128)} %bitcast.6, f32[]{:T(128)} %bitcast.5, f32[]{:T(128)} %bitcast.4, f32[]{:T(128)} %bitcast.3, ...), kind=kOutput, calls=%fused_computation.231 | convolution fusion | flops 1585151 | bytes 55776 | tf_op jit(solution)/shard_map/dot_general | solution.py:37
  320.0 43.0 %psum.53 = f32[]{:T(128)} all-reduce(f32[]{:T(128)} %get-tuple-element.10), channel_id=1, replica_groups=mesh['day'=2,'stu'=16] {'day','stu'}, use_global_device_ids=true, to_apply=%region_10.0 | all-reduce | flops 1 | bytes 8 | tf_op jit(solution)/shard_map/psum | solution.py:50
  364.2 0.6 multiply_reduce_fusion.1
  364.8 39.0 %psum.54 = f32[]{:T(128)} all-reduce(f32[]{:T(128)} %get-tuple-element.8), channel_id=1, replica_groups=mesh['day'=2,'stu'=16] {'day','stu'}, use_global_device_ids=true, to_apply=%region_12.0 | all-reduce | flops 1 | bytes 8 | tf_op jit(solution)/shard_map/psum | solution.py:50
  405.2 0.1 slice.411
  405.3 1.3 collective-permute-start.6
  406.5 4.2 collective-permute-done.6
  410.8 4.5 fusion.20
  415.3 1.6 collective-permute-start.7
  416.9 17.6 %all_gather.15 = f32[32,256]{0,1:T(8,128)S(1)} all-gather(f32[32,16]{0,1:T(8,128)S(1)} %multiply_add_fusion.1), channel_id=1, replica_groups=mesh['day'=2,'stu'=16] {'stu'}, dimensions={1}, use_global_device_ids=true | all-gather | bytes 34816 | tf_op jit(solution)/shard_map/all_gather | solution.py:38
  434.5 5.1 %multiply_reduce_fusion = (f32[]{:T(128)}, f32[32,16]{0,1:T(8,128)S(1)}) fusion(f32[32,16]{0,1:T(8,128)S(1)} %multiply_add_fusion.1, f32[7,16]{0,1:T(8,128)S(1)} %collective-permute-done.7, f32[32,16]{0,1:T(8,128)S(1)} %fusion.20, f32[]{:T(128)} %bitcast.7, f32[]{:T(128)} %bitcast.6, f32[]{:T(128)} %bitcast.5, f32[]{:T(128)} %bitcast.4, f32[]{:T(128)} %bitcast.3, ...), kind=kOutput, calls=%fused_computation.227 | convolution fusion | flops 1585151 | bytes 55776 | tf_op jit(solution)/shard_map/dot_general | solution.py:37
  439.7 43.2 %psum.55 = f32[]{:T(128)} all-reduce(f32[]{:T(128)} %get-tuple-element.6), channel_id=1, replica_groups=mesh['day'=2,'stu'=16] {'day','stu'}, use_global_device_ids=true, to_apply=%region_14.0 | all-reduce | flops 1 | bytes 8 | tf_op jit(solution)/shard_map/psum | solution.py:50
  484.3 0.6 multiply_subtract_fusion
  (17 shorter events, 0.1 us)
Async XLA Ops:
  7.2 4.8 copy-start
  7.2 4.8 copy-start.1
  7.2 95.9 %all-reduce.3.cloned.1.call-start = ((), (), s32[]{:S(2)}) async-start(), calls=%async_computation.2 | async-start | bytes 524288 | tf_op jit(solution)/shard_map/psum | solution.py:54
  8.3 21.6 %collective-permute-start = (f32[7,16]{0,1:T(8,128)S(1)}, f32[7,16]{0,1:T(8,128)S(1)}, u32[]{:S(2)}, u32[]{:S(2)}) collective-permute-start(f32[7,16]{0,1:T(8,128)S(1)} %slice.333), channel_id=1, source_target_pairs={{0,16},{1,17},{2,18},{3,19},{4,20},{5,21},{6,22},{7,23},{8,24},{9,... | collective-permute-start | bytes 1352 | tf_op jit(solution)/shard_map/ppermute | solution.py:14
  11.2 0.7 copy-start.2
  11.3 150.2 %reduce-scatter.2.cloned.1.call-start = ((), (), s32[]{:S(2)}) async-start(), calls=%async_computation.1 | async-start | bytes 139264 | tf_op jit(solution)/shard_map/reduce_scatter | solution.py:72
  13.0 0.7 copy-start.3
  34.3 69.5 %collective-permute-start.1 = (f32[7,16]{0,1:T(8,128)S(1)}, f32[7,16]{0,1:T(8,128)S(1)}, u32[]{:S(2)}, u32[]{:S(2)}) collective-permute-start(f32[7,16]{0,1:T(8,128)S(1)} %bitcast.27), channel_id=1, source_target_pairs={{16,0},{17,1},{18,2},{19,3},{20,4},{21,5},{22,6},{23,7},{24,8},{25... | collective-permute-start | bytes 1352 | tf_op jit(solution)/shard_map/ppermute | solution.py:14
  166.8 5.5 %collective-permute-start.2 = (f32[7,16]{0,1:T(8,128)S(1)}, f32[7,16]{0,1:T(8,128)S(1)}, u32[]{:S(2)}, u32[]{:S(2)}) collective-permute-start(f32[7,16]{0,1:T(8,128)S(1)} %slice.359), channel_id=1, source_target_pairs={{0,16},{1,17},{2,18},{3,19},{4,20},{5,21},{6,22},{7,23},{8,24},{9,... | collective-permute-start | bytes 1352 | tf_op jit(solution)/shard_map/ppermute | solution.py:14
  176.8 17.0 %collective-permute-start.3 = (f32[7,16]{0,1:T(8,128)S(1)}, f32[7,16]{0,1:T(8,128)S(1)}, u32[]{:S(2)}, u32[]{:S(2)}) collective-permute-start(f32[7,16]{0,1:T(8,128)S(1)} %bitcast.29), channel_id=1, source_target_pairs={{16,0},{17,1},{18,2},{19,3},{20,4},{21,5},{22,6},{23,7},{24,8},{25... | collective-permute-start | bytes 1352 | tf_op jit(solution)/shard_map/ppermute | solution.py:14
  285.1 5.5 %collective-permute-start.4 = (f32[7,16]{0,1:T(8,128)S(1)}, f32[7,16]{0,1:T(8,128)S(1)}, u32[]{:S(2)}, u32[]{:S(2)}) collective-permute-start(f32[7,16]{0,1:T(8,128)S(1)} %slice.385), channel_id=1, source_target_pairs={{0,16},{1,17},{2,18},{3,19},{4,20},{5,21},{6,22},{7,23},{8,24},{9,... | collective-permute-start | bytes 1352 | tf_op jit(solution)/shard_map/ppermute | solution.py:14
  295.1 19.6 %collective-permute-start.5 = (f32[7,16]{0,1:T(8,128)S(1)}, f32[7,16]{0,1:T(8,128)S(1)}, u32[]{:S(2)}, u32[]{:S(2)}) collective-permute-start(f32[7,16]{0,1:T(8,128)S(1)} %bitcast.30), channel_id=1, source_target_pairs={{16,0},{17,1},{18,2},{19,3},{20,4},{21,5},{22,6},{23,7},{24,8},{25... | collective-permute-start | bytes 1352 | tf_op jit(solution)/shard_map/ppermute | solution.py:14
  405.3 5.5 %collective-permute-start.6 = (f32[7,16]{0,1:T(8,128)S(1)}, f32[7,16]{0,1:T(8,128)S(1)}, u32[]{:S(2)}, u32[]{:S(2)}) collective-permute-start(f32[7,16]{0,1:T(8,128)S(1)} %slice.411), channel_id=1, source_target_pairs={{0,16},{1,17},{2,18},{3,19},{4,20},{5,21},{6,22},{7,23},{8,24},{9,... | collective-permute-start | bytes 1352 | tf_op jit(solution)/shard_map/ppermute | solution.py:14
  415.3 19.3 %collective-permute-start.7 = (f32[7,16]{0,1:T(8,128)S(1)}, f32[7,16]{0,1:T(8,128)S(1)}, u32[]{:S(2)}, u32[]{:S(2)}) collective-permute-start(f32[7,16]{0,1:T(8,128)S(1)} %bitcast.28), channel_id=1, source_target_pairs={{16,0},{17,1},{18,2},{19,3},{20,4},{21,5},{22,6},{23,7},{24,8},{25... | collective-permute-start | bytes 1352 | tf_op jit(solution)/shard_map/ppermute | solution.py:14
Sparse Core Ops, SparseCore 0:
  11.4 91.6 all-reduce.2
  106.5 54.8 reduce-scatter.1
where the time goes:
time: 494 us; the launch traced here: 492 us
  blocking collectives  274 us (55%)
  waiting for transfers between devices  135 us (27%)
  matrix products  23.1 us (5%)
  between operations  20.9 us (4%)
  other arithmetic  20.4 us (4%)
  starting transfers between devices  14.7 us (3%)
    psum x5, blocking collectives, global_total(): return lax.psum(value, ('day', 'stu'))  208 us
    all_gather x4, blocking collectives, with_gram(): lax.all_gather(values, 'stu', axis=1, tiled=True)  66.5 us
    psum x1, waiting for transfers between devices, summed_gram(): return lax.psum(local_gram, 'stu')  64.2 us
    reduce_scatter x1, waiting for transfers between devices, local(): lax.psum_scatter(local_terms, 'stu', scatter_dimension=1, tiled=True)  57.7 us
    dot_general x4, matrix products, with_gram(): jnp.dot(lax.all_gather(values, 'stu', axis=1, tiled=True), gram_part, pre...  20.8 us
    sub x4, other arithmetic, filter_rows(): out = out - coef[lag - 1] * extended[LAGS - lag:LAGS - lag + count]  17.8 us
    ppermute x8, starting transfers between devices, shifted(): return lax.ppermute(block, axis, route)  14.6 us
    ppermute x8, waiting for transfers between devices, shifted(): return lax.ppermute(block, axis, route)  12.7 us
  transfers between devices with their start and end apart: 10, of which 5 were waited for; matrix products, arithmetic and copies ran while one was open for 2% of the time, Pallas kernels for 0%

commit v1 on v0

--- a/solution.py
+++ b/solution.py
@@ -51,7 +51,7 @@
 
 
 def summed_gram(local_gram):
-    return lax.psum(local_gram, "stu")
+    return jnp.sum(jax.lax.all_gather(local_gram, axis_name="stu"), axis=0)
 
 
 def local(performance, student_factor, skill_factor, day_prev, ar_coef):

time: 494 us -> 452 us (0.915)
  waiting for transfers between devices: 135 us -> 88.6 us
    psum x1 -> x0, waiting for transfers between devices: 64.2 us -> none  [summed_gram(): return lax.psum(local_gram, 'stu')]
    all_gather x0 -> x1, waiting for transfers between devices: none -> 20.6 us  [summed_gram(): return jnp.sum(jax.lax.all_gather(local_gram, axis_name='stu'), axis=0)]
  transfers between devices with their start and end apart: 10 -> 10, of which waited for: 5 -> 5; matrix products, arithmetic and copies ran while one was open for 2% -> 3% of each run, Pallas kernels for 0% -> 0%
where the time goes in v1:
time: 452 us; the launch traced here: 450 us
  blocking collectives  274 us (61%)
  waiting for transfers between devices  88.6 us (20%)
  matrix products  24.6 us (5%)
  other arithmetic  23.3 us (5%)
  between operations  20.9 us (5%)
  starting transfers between devices  14.7 us (3%)
    psum x5, blocking collectives, global_total(): return lax.psum(value, ('day', 'stu'))  208 us
    all_gather x4, blocking collectives, with_gram(): lax.all_gather(values, 'stu', axis=1, tiled=True)  66.6 us
    reduce_scatter x1, waiting for transfers between devices, local(): lax.psum_scatter(local_terms, 'stu', scatter_dimension=1, tiled=True)  55.2 us
    dot_general x4, matrix products, with_gram(): jnp.dot(lax.all_gather(values, 'stu', axis=1, tiled=True), gram_part, pre...  21.2 us
    all_gather x1, waiting for transfers between devices, summed_gram(): return jnp.sum(jax.lax.all_gather(local_gram, axis_name='stu'), axis=0)  20.6 us
    sub x4, other arithmetic, filter_rows(): out = out - coef[lag - 1] * extended[LAGS - lag:LAGS - lag + count]  18.3 us
    ppermute x8, starting transfers between devices, shifted(): return lax.ppermute(block, axis, route)  14.6 us
    ppermute x8, waiting for transfers between devices, shifted(): return lax.ppermute(block, axis, route)  12.8 us
  transfers between devices with their start and end apart: 10, of which 5 were waited for; matrix products, arithmetic and copies ran while one was open for 3% of the time, Pallas kernels for 0%

profile of v1, /device:TPU:14, one launch (start us, length us, event | category | flops | bytes accessed | tf_op | source)
XLA Modules:
  0.0 450.1 jit_solution(7622981522461853916)
XLA Ops:
  7.2 1.7 fusion.139
  9.0 0.8 constant_dynamic-slice_fusion.1
  9.8 0.1 copy.11
  9.8 0.1 slice.333
  9.9 1.3 collective-permute-start
  11.2 0.7 convert_element_type.3
  11.9 1.4 fusion
  13.3 0.8 copy.9
  14.1 0.3 fusion.140
  14.4 1.6 fusion.138
  16.0 15.6 %all_gather.18 = f32[32,256]{0,1:T(8,128)S(1)} all-gather(f32[32,16]{0,1:T(8,128)S(1)} %copy.11), channel_id=1, replica_groups=mesh['day'=2,'stu'=16] {'stu'}, dimensions={1}, use_global_device_ids=true | all-gather | bytes 34816 | tf_op jit(solution)/shard_map/all_gather | solution.py:38
  31.6 4.6 %fusion.120 = f32[32,16]{0,1:T(8,128)S(1)} fusion(f32[32,16]{0,1:T(8,128)S(1)} %copy.11, f32[7,16]{0,1:T(8,128)S(1)} %collective-permute-done, f32[]{:T(128)} %bitcast.8, f32[]{:T(128)} %bitcast.7, f32[]{:T(128)} %bitcast.6, f32[]{:T(128)} %bitcast.5, f32[]{:T(128)} %bitcast.4, f32[]{:T(128)} %bitcast.3, f32[]{:T(128)} %bitcast.2), kind=kLoop, calls=%fused_computation.200 | loop fusion | flops 10752 | bytes 4572 | tf_op jit(solution)/shard_map/sub | solution.py:20
  36.2 4.5 collective-permute-start.1
  40.7 20.6 %all-gather.3.cloned.1.call-done = f32[4096,256]{1,0:T(8,128)} async-done(((f32[256,256]{1,0:T(8,128)}), f32[4096,256]{1,0:T(8,128)}) %all-gather.3.cloned.1.call-update) | async-done | bytes 4194320 | tf_op jit(solution)/shard_map/all_gather | solution.py:54
  61.3 2.5 reduce_sum.73
  63.7 0.1 constant_dynamic-slice_fusion
  63.9 0.1 copy.12
  63.9 55.2 %reduce-scatter.2.cloned.1.call-done = f32[32,16]{0,1:T(8,128)} async-done(((f32[32,256]{0,1:T(8,128)}), f32[32,16]{0,1:T(8,128)}) %reduce-scatter.2.cloned.1.call-update) | async-done | bytes 2064 | tf_op jit(solution)/shard_map/reduce_scatter | solution.py:72
  119.2 5.3 %fusion.104 = f32[32,16]{0,1:T(8,128)S(1)} fusion(f32[32,16]{0,1:T(8,128)} %reduce-scatter.2.cloned.1.call-done, f32[7,16]{0,1:T(8,128)S(1)} %collective-permute-done.1, f32[32,16]{0,1:T(8,128)S(1)} %fusion.120, f32[]{:T(128)} %bitcast.8, f32[]{:T(128)} %bitcast.7, f32[]{:T(128)} %bitcast.6, f32[]{:T(128)} %bitcast.5, f32[]{:T(128)} %bitcast.4, ...), kind=kOutput, calls=%fused_computation.173 | convolution fusion | flops 1584640 | bytes 55772 | tf_op jit(solution)/shard_map/dot_general | solution.py:37
  124.5 0.1 slice.359
  124.6 1.3 collective-permute-start.2
  125.9 4.2 collective-permute-done.2
  130.1 4.6 %fusion.86 = f32[32,16]{0,1:T(8,128)S(1)} fusion(f32[32,16]{0,1:T(8,128)S(1)} %fusion.104, f32[7,16]{0,1:T(8,128)S(1)} %collective-permute-done.2, f32[]{:T(128)} %bitcast.8, f32[]{:T(128)} %bitcast.7, f32[]{:T(128)} %bitcast.6, f32[]{:T(128)} %bitcast.5, f32[]{:T(128)} %bitcast.4, f32[]{:T(128)} %bitcast.3, f32[]{:T(128)} %bitcast.2), kind=kLoop, calls=%fused_computation.144 | loop fusion | flops 10752 | bytes 4572 | tf_op jit(solution)/shard_map/sub | solution.py:20
  134.7 1.6 collective-permute-start.3
  136.4 15.4 %all_gather.21 = f32[32,256]{0,1:T(8,128)S(1)} all-gather(f32[32,16]{0,1:T(8,128)S(1)} %fusion.104), channel_id=1, replica_groups=mesh['day'=2,'stu'=16] {'stu'}, dimensions={1}, use_global_device_ids=true | all-gather | bytes 34816 | tf_op jit(solution)/shard_map/all_gather | solution.py:38
  151.7 5.3 %multiply_reduce_fusion.4 = (f32[]{:T(128)}, f32[]{:T(128)}, f32[32,16]{0,1:T(8,128)S(1)}) fusion(f32[32,16]{0,1:T(8,128)S(1)} %fusion.104, f32[7,16]{0,1:T(8,128)S(1)} %collective-permute-done.3, f32[32,16]{0,1:T(8,128)S(1)} %fusion.86, f32[]{:T(128)} %bitcast.8, f32[]{:T(128)} %bitcast.7, f32[]{:T(128)} %bitcast.6, f32[]{:T(128)} %bitcast.5, ...), kind=kOutput, calls=%fused_computation.235 | convolution fusion | flops 1586174 | bytes 55780 | tf_op jit(solution)/shard_map/dot_general | solution.py:37
  157.0 44.0 %all-reduce = (f32[]{:T(128)}, f32[]{:T(128)}) all-reduce(f32[]{:T(128)} %get-tuple-element.3, f32[]{:T(128)} %get-tuple-element.2), channel_id=1, replica_groups=mesh['day'=2,'stu'=16] {'day','stu'}, use_global_device_ids=true, to_apply=%region_4.0 | all-reduce | flops 2 | bytes 16 | tf_op jit(solution)/shard_map/psum | solution.py:50
  202.4 0.6 multiply_reduce_fusion.3
  203.1 38.6 %psum.44 = f32[]{:T(128)} all-reduce(f32[]{:T(128)} %multiply_reduce_fusion.3), channel_id=1, replica_groups=mesh['day'=2,'stu'=16] {'day','stu'}, use_global_device_ids=true, to_apply=%region_8.0 | all-reduce | flops 1 | bytes 8 | tf_op jit(solution)/shard_map/psum | solution.py:50
  243.0 0.1 slice.385
  243.1 1.3 collective-permute-start.4
  244.4 4.2 collective-permute-done.4
  248.6 4.6 %fusion.53 = f32[32,16]{0,1:T(8,128)S(1)} fusion(f32[32,16]{0,1:T(8,128)S(1)} %multiply_add_fusion.2, f32[7,16]{0,1:T(8,128)S(1)} %collective-permute-done.4, f32[]{:T(128)} %bitcast.8, f32[]{:T(128)} %bitcast.7, f32[]{:T(128)} %bitcast.6, f32[]{:T(128)} %bitcast.5, f32[]{:T(128)} %bitcast.4, f32[]{:T(128)} %bitcast.3, f32[]{:T(128)} %bitcast.2), kind=kLoop, calls=%fused_computation.89 | loop fusion | flops 10752 | bytes 4572 | tf_op jit(solution)/shard_map/sub | solution.py:20
  253.2 1.6 collective-permute-start.5
  254.9 18.0 %all_gather.22 = f32[32,256]{0,1:T(8,128)S(1)} all-gather(f32[32,16]{0,1:T(8,128)S(1)} %multiply_add_fusion.2), channel_id=1, replica_groups=mesh['day'=2,'stu'=16] {'stu'}, dimensions={1}, use_global_device_ids=true | all-gather | bytes 34816 | tf_op jit(solution)/shard_map/all_gather | solution.py:38
  272.8 5.3 %multiply_reduce_fusion.2 = (f32[]{:T(128)}, f32[32,16]{0,1:T(8,128)S(1)}) fusion(f32[32,16]{0,1:T(8,128)S(1)} %multiply_add_fusion.2, f32[7,16]{0,1:T(8,128)S(1)} %collective-permute-done.5, f32[32,16]{0,1:T(8,128)S(1)} %fusion.53, f32[]{:T(128)} %bitcast.8, f32[]{:T(128)} %bitcast.7, f32[]{:T(128)} %bitcast.6, f32[]{:T(128)} %bitcast.5, f32[]{:T(128)} %bitcast.4, ...), kind=kOutput, calls=%fused_computation.231 | convolution fusion | flops 1585151 | bytes 55776 | tf_op jit(solution)/shard_map/dot_general | solution.py:37
  278.2 43.0 %psum.45 = f32[]{:T(128)} all-reduce(f32[]{:T(128)} %get-tuple-element.10), channel_id=1, replica_groups=mesh['day'=2,'stu'=16] {'day','stu'}, use_global_device_ids=true, to_apply=%region_10.0 | all-reduce | flops 1 | bytes 8 | tf_op jit(solution)/shard_map/psum | solution.py:50
  322.4 0.6 multiply_reduce_fusion.1
  323.0 39.0 %psum.46 = f32[]{:T(128)} all-reduce(f32[]{:T(128)} %get-tuple-element.8), channel_id=1, replica_groups=mesh['day'=2,'stu'=16] {'day','stu'}, use_global_device_ids=true, to_apply=%region_12.0 | all-reduce | flops 1 | bytes 8 | tf_op jit(solution)/shard_map/psum | solution.py:50
  363.3 0.1 slice.411
  363.4 1.3 collective-permute-start.6
  364.7 4.2 collective-permute-done.6
  368.9 4.6 %fusion.20 = f32[32,16]{0,1:T(8,128)S(1)} fusion(f32[32,16]{0,1:T(8,128)S(1)} %multiply_add_fusion.1, f32[7,16]{0,1:T(8,128)S(1)} %collective-permute-done.6, f32[]{:T(128)} %bitcast.8, f32[]{:T(128)} %bitcast.7, f32[]{:T(128)} %bitcast.6, f32[]{:T(128)} %bitcast.5, f32[]{:T(128)} %bitcast.4, f32[]{:T(128)} %bitcast.3, f32[]{:T(128)} %bitcast.2), kind=kLoop, calls=%fused_computation.34 | loop fusion | flops 10752 | bytes 4572 | tf_op jit(solution)/shard_map/sub | solution.py:20
  373.5 1.6 collective-permute-start.7
  375.2 17.6 %all_gather.23 = f32[32,256]{0,1:T(8,128)S(1)} all-gather(f32[32,16]{0,1:T(8,128)S(1)} %multiply_add_fusion.1), channel_id=1, replica_groups=mesh['day'=2,'stu'=16] {'stu'}, dimensions={1}, use_global_device_ids=true | all-gather | bytes 34816 | tf_op jit(solution)/shard_map/all_gather | solution.py:38
  392.8 5.3 %multiply_reduce_fusion = (f32[]{:T(128)}, f32[32,16]{0,1:T(8,128)S(1)}) fusion(f32[32,16]{0,1:T(8,128)S(1)} %multiply_add_fusion.1, f32[7,16]{0,1:T(8,128)S(1)} %collective-permute-done.7, f32[32,16]{0,1:T(8,128)S(1)} %fusion.20, f32[]{:T(128)} %bitcast.8, f32[]{:T(128)} %bitcast.7, f32[]{:T(128)} %bitcast.6, f32[]{:T(128)} %bitcast.5, f32[]{:T(128)} %bitcast.4, ...), kind=kOutput, calls=%fused_computation.227 | convolution fusion | flops 1585151 | bytes 55776 | tf_op jit(solution)/shard_map/dot_general | solution.py:37
  398.0 43.2 %psum.47 = f32[]{:T(128)} all-reduce(f32[]{:T(128)} %get-tuple-element.6), channel_id=1, replica_groups=mesh['day'=2,'stu'=16] {'day','stu'}, use_global_device_ids=true, to_apply=%region_14.0 | all-reduce | flops 1 | bytes 8 | tf_op jit(solution)/shard_map/psum | solution.py:50
  442.6 0.6 multiply_subtract_fusion
  (14 shorter events, 0.2 us)
Async XLA Ops:
  7.2 4.7 %copy-start = (bf16[1024,256]{1,0:T(8,128)(2,1)S(1)}, bf16[1024,256]{1,0:T(8,128)(2,1)}, u32[]{:S(2)}) copy-start(bf16[1024,256]{1,0:T(8,128)(2,1)} %param.7) | copy-start | bytes 1572868
  7.2 54.1 %all-gather.3.cloned.1.call-start = ((), (), s32[]{:S(2)}) async-start(), calls=%async_computation.2 | async-start | bytes 4456448 | tf_op jit(solution)/shard_map/all_gather | solution.py:54
  8.9 110.2 %reduce-scatter.2.cloned.1.call-start = ((), (), s32[]{:S(2)}) async-start(), calls=%async_computation.1 | async-start | bytes 139264 | tf_op jit(solution)/shard_map/reduce_scatter | solution.py:72
  9.9 21.7 %collective-permute-start = (f32[7,16]{0,1:T(8,128)S(1)}, f32[7,16]{0,1:T(8,128)S(1)}, u32[]{:S(2)}, u32[]{:S(2)}) collective-permute-start(f32[7,16]{0,1:T(8,128)S(1)} %slice.333), channel_id=1, source_target_pairs={{0,16},{1,17},{2,18},{3,19},{4,20},{5,21},{6,22},{7,23},{8,24},{9,... | collective-permute-start | bytes 1352 | tf_op jit(solution)/shard_map/ppermute | solution.py:14
  36.2 27.7 %collective-permute-start.1 = (f32[7,16]{0,1:T(8,128)S(1)}, f32[7,16]{0,1:T(8,128)S(1)}, u32[]{:S(2)}, u32[]{:S(2)}) collective-permute-start(f32[7,16]{0,1:T(8,128)S(1)} %bitcast.29), channel_id=1, source_target_pairs={{16,0},{17,1},{18,2},{19,3},{20,4},{21,5},{22,6},{23,7},{24,8},{25... | collective-permute-start | bytes 1352 | tf_op jit(solution)/shard_map/ppermute | solution.py:14
  124.6 5.5 %collective-permute-start.2 = (f32[7,16]{0,1:T(8,128)S(1)}, f32[7,16]{0,1:T(8,128)S(1)}, u32[]{:S(2)}, u32[]{:S(2)}) collective-permute-start(f32[7,16]{0,1:T(8,128)S(1)} %slice.359), channel_id=1, source_target_pairs={{0,16},{1,17},{2,18},{3,19},{4,20},{5,21},{6,22},{7,23},{8,24},{9,... | collective-permute-start | bytes 1352 | tf_op jit(solution)/shard_map/ppermute | solution.py:14
  134.7 17.0 %collective-permute-start.3 = (f32[7,16]{0,1:T(8,128)S(1)}, f32[7,16]{0,1:T(8,128)S(1)}, u32[]{:S(2)}, u32[]{:S(2)}) collective-permute-start(f32[7,16]{0,1:T(8,128)S(1)} %bitcast.31), channel_id=1, source_target_pairs={{16,0},{17,1},{18,2},{19,3},{20,4},{21,5},{22,6},{23,7},{24,8},{25... | collective-permute-start | bytes 1352 | tf_op jit(solution)/shard_map/ppermute | solution.py:14
  243.1 5.5 %collective-permute-start.4 = (f32[7,16]{0,1:T(8,128)S(1)}, f32[7,16]{0,1:T(8,128)S(1)}, u32[]{:S(2)}, u32[]{:S(2)}) collective-permute-start(f32[7,16]{0,1:T(8,128)S(1)} %slice.385), channel_id=1, source_target_pairs={{0,16},{1,17},{2,18},{3,19},{4,20},{5,21},{6,22},{7,23},{8,24},{9,... | collective-permute-start | bytes 1352 | tf_op jit(solution)/shard_map/ppermute | solution.py:14
  253.2 19.6 %collective-permute-start.5 = (f32[7,16]{0,1:T(8,128)S(1)}, f32[7,16]{0,1:T(8,128)S(1)}, u32[]{:S(2)}, u32[]{:S(2)}) collective-permute-start(f32[7,16]{0,1:T(8,128)S(1)} %bitcast.32), channel_id=1, source_target_pairs={{16,0},{17,1},{18,2},{19,3},{20,4},{21,5},{22,6},{23,7},{24,8},{25... | collective-permute-start | bytes 1352 | tf_op jit(solution)/shard_map/ppermute | solution.py:14
  363.4 5.5 %collective-permute-start.6 = (f32[7,16]{0,1:T(8,128)S(1)}, f32[7,16]{0,1:T(8,128)S(1)}, u32[]{:S(2)}, u32[]{:S(2)}) collective-permute-start(f32[7,16]{0,1:T(8,128)S(1)} %slice.411), channel_id=1, source_target_pairs={{0,16},{1,17},{2,18},{3,19},{4,20},{5,21},{6,22},{7,23},{8,24},{9,... | collective-permute-start | bytes 1352 | tf_op jit(solution)/shard_map/ppermute | solution.py:14
  373.5 19.3 %collective-permute-start.7 = (f32[7,16]{0,1:T(8,128)S(1)}, f32[7,16]{0,1:T(8,128)S(1)}, u32[]{:S(2)}, u32[]{:S(2)}) collective-permute-start(f32[7,16]{0,1:T(8,128)S(1)} %bitcast.30), channel_id=1, source_target_pairs={{16,0},{17,1},{18,2},{19,3},{20,4},{21,5},{22,6},{23,7},{24,8},{25... | collective-permute-start | bytes 1352 | tf_op jit(solution)/shard_map/ppermute | solution.py:14
Sparse Core Ops, SparseCore 0:
  10.2 51.0 all-gather.2
  64.7 54.3 reduce-scatter.1
